TPU v7x, 512 devices: a whole 4x4x16 slice. The times are simulated.
512 devices in a mesh: dom: 64 (over z, y), src: 4 (over x), rel: 2 (over core).
Axes of the slice: x: 4, y: 4, z: 16, core: 2. Of those that a mesh axis runs over, the one named last changes fastest.
Arguments:
- source_feats: bfloat16 [131072, 256], P(('dom', 'src', 'rel')), may hold values from -6 to 6
- rel_weight: bfloat16 [12, 256, 256], P('rel'), may hold values from -0.375 to 0.375
- halo_pick: int32 [64, 4, 2, 64], P('dom', 'src', 'rel'), may hold values from 0 to 1
- entry_index: int32 [64, 4, 2, 3, 64], P('dom', 'src', 'rel'), may hold values from 0 to 63, as said below
- entry_count: int32 [64, 4, 2], P('dom', 'src', 'rel'), may hold values from 1 to 64, as said below
- entry_values: bfloat16 [64, 4, 2, 64, 128, 128], P('dom', 'src', 'rel'), may hold values from -0.125 to 0.125
- cotangent: bfloat16 [131072, 256], P(('dom', 'src', 'rel')), may hold values from -0.0546875 to 0.0546875
Outputs:
- out_feats: bfloat16 [131072, 256], P(('dom', 'src', 'rel'))
- grad_rel: float32 [12, 256, 256], P('rel')
Inputs may be any that keep to these rules, and one draw needn't show every extreme that they name: `entry_index`: row 0 of an entry is a target block below 16, row 1 a partition below 64, row 2 a relation below 6. Over all 64 entries of one (p,s,g), every partition is named 64 // 64 times or once more. `entry_count`: live entries come first; some (p,s,g) has all 64 entries live in every draw.
All inputs are finite; a program needn't handle non-finite values.
Results may differ from a plain program's by a relative error of at most 0.0057.
Values may be sent and summed in bfloat16 or wider, within the bound.
A program may use at most 64 MiB of HBM per device.

v0:
```python
import jax
import jax.numpy as jnp
from jax import lax
from jax.sharding import PartitionSpec as P


def silu_slope(pre_values):
    logistic = jax.nn.sigmoid(pre_values)
    return logistic * (1.0 + pre_values * (1.0 - logistic))


def local(source_feats, rel_weight, halo_pick, entry_index, entry_count, entry_values, cotangent):
    partitions = lax.axis_size("dom")
    tile_rows = entry_values.shape[-1]
    features = source_feats.shape[1]
    chosen = halo_pick.reshape(-1)
    everyone = lax.all_gather(source_feats, "dom", axis=0, tiled=True)
    everyone = everyone.reshape(partitions, -1, tile_rows, features)
    halo_blocks = everyone[jnp.arange(partitions, dtype=jnp.int32), chosen]
    own_rows = cotangent.shape[0]
    tgt_blocks = own_rows * lax.axis_size("src") * lax.axis_size("rel") // tile_rows
    rel_local = rel_weight.shape[0]
    entry_table = entry_index.reshape(3, -1)
    slot_total = entry_table.shape[1]
    values = entry_values.reshape(-1, tile_rows, tile_rows)
    picked = halo_blocks[entry_table[1]]
    messages = jnp.einsum("eij,ejd->eid", values, picked, preferred_element_type=jnp.float32)
    live_mask = jnp.arange(slot_total, dtype=jnp.int32) < entry_count.reshape(())
    target_slot = entry_table[2] * tgt_blocks + entry_table[0]
    slot_numbers = jnp.arange(rel_local * tgt_blocks, dtype=jnp.int32)
    placement = ((slot_numbers[:, None] == target_slot[None, :]) & live_mask[None, :]).astype(
        jnp.float32
    )
    totals = jnp.einsum(
        "se,eid->sid",
        placement,
        messages,
        precision=lax.Precision.HIGHEST,
        preferred_element_type=jnp.float32,
    )
    relation_terms = totals.astype(jnp.bfloat16).reshape(
        rel_local, tgt_blocks * tile_rows, features
    )
    summed = lax.psum_scatter(
        jnp.einsum("rtd,rde->te", relation_terms, rel_weight, preferred_element_type=jnp.float32),
        ("src", "rel"),
        scatter_dimension=0,
        tiled=True,
    )
    out_feats = jax.nn.silu(summed).astype(jnp.bfloat16)
    local_grad = (cotangent.astype(jnp.float32) * silu_slope(summed)).astype(jnp.bfloat16)
    grad_rows = lax.all_gather(local_grad, ("src", "rel"), axis=0, tiled=True)
    weight_terms = jnp.einsum(
        "rtd,te->rde", relation_terms, grad_rows, preferred_element_type=jnp.float32
    )
    grad_rel = lax.psum(weight_terms, ("dom", "src"))
    return (out_feats, grad_rel)


def solution(mesh):
    return jax.shard_map(
        local,
        mesh=mesh,
        in_specs=(
            P(("dom", "src", "rel"), None),
            P("rel", None, None),
            P("dom", "src", "rel", None),
            P("dom", "src", "rel", None, None),
            P("dom", "src", "rel"),
            P("dom", "src", "rel", None, None, None),
            P(("dom", "src", "rel"), None),
        ),
        out_specs=(P(("dom", "src", "rel"), None), P("rel", None, None)),
        check_vma=False,
    )
```

profile of v0, /device:TPU:2, one launch (start us, length us, event | category | flops | bytes accessed | tf_op | source)
XLA Modules:
  0.0 711.4 jit_solution(15321850771566686382)
XLA Ops:
  7.2 0.0 copy-start
  7.2 0.0 all-gather.3.cloned.1.call-start
  7.2 0.7 all-gather.3.cloned.1.call-update
  7.9 0.0 reduce-scatter.2.cloned.1.call-start
  8.6 0.7 fusion.17
  9.3 0.7 add_bitcast_fusion
  10.0 0.7 fusion.18
  10.6 160.9 %all-gather.3.cloned.1.call-done = bf16[16384,256]{1,0:T(8,128)(2,1)} async-done(((bf16[256,256]{1,0:T(8,128)(2,1)}), bf16[16384,256]{1,0:T(8,128)(2,1)}) %all-gather.3.cloned.1.call-update) | async-done | bytes 8388624 | tf_op jit(solution)/shard_map/all_gather | solution.py:17
  171.5 6.2 gather_fusion
  177.7 4.9 gather_fusion.1
  182.6 0.0 copy-done
  182.6 6.7 fusion.5
  189.3 9.2 %copy.12 = f32[64,256,128]{1,0,2:T(8,128)} copy(f32[64,256,128]{2,1,0:T(8,128)} %fusion.5) | data formatting | bytes 16777216 | tf_op jit(solution)/shard_map/eij,ejd->eid/dot_general | solution.py:27
  198.5 8.4 %fusion.2 = bf16[96,128,256]{2,0,1:T(8,128)(2,1)S(1)} fusion(f32[64,256,128]{1,0,2:T(8,128)} %copy.12, s32[64]{0:T(128)S(1)} %add_bitcast_fusion, pred[64]{0:T(512)(128)(4,1)S(1)} %iota_compare_fusion.1), kind=kOutput, calls=%fused_computation.4 | convolution fusion | flops 2419077120 | bytes 14680384 | tf_op jit(solution)/shard_map/se,eid->sid/dot_general | solution.py:34
  207.0 0.0 copy-start.3
  207.0 3.7 copy.10
  210.6 0.0 copy-start.1
  210.6 2.6 copy-done.1
  213.3 0.0 copy-done.3
  213.3 3.3 convolution_bitcast_fusion
  216.5 0.0 reduce-scatter.2.cloned.1.call-update
  216.6 0.0 all-gather.5.cloned.1.call-start
  216.6 33.4 %reduce-scatter.2.cloned.1.call-done = f32[256,256]{1,0:T(8,128)} async-done(((f32[2048,256]{1,0:T(8,128)}), f32[256,256]{1,0:T(8,128)}) %reduce-scatter.2.cloned.1.call-update) | async-done | bytes 262160 | tf_op jit(solution)/shard_map/reduce_scatter | solution.py:44
  250.0 0.0 copy-done.2
  250.0 1.8 multiply_convert_fusion
  251.7 0.0 all-gather.5.cloned.1.call-update
  251.8 0.0 all-reduce.2.cloned.1.call-start
  251.8 32.6 %all-gather.5.cloned.1.call-done = bf16[2048,256]{1,0:T(8,128)(2,1)} async-done(((bf16[256,256]{1,0:T(8,128)(2,1)}), bf16[2048,256]{1,0:T(8,128)(2,1)}) %all-gather.5.cloned.1.call-update) | async-done | bytes 1048592 | tf_op jit(solution)/shard_map/all_gather | solution.py:52
  284.4 6.0 fusion.7
  290.4 0.0 all-reduce.2.cloned.1.call-update
  290.4 411.6 %all-reduce.2.cloned.1.call-done = f32[6,256,256]{2,1,0:T(8,128)} async-done(((f32[6,256,256]{2,1,0:T(8,128)}), f32[6,256,256]{2,1,0:T(8,128)}) %all-reduce.2.cloned.1.call-update) | async-done | bytes 1572880 | tf_op jit(solution)/shard_map/psum | solution.py:56
  702.1 2.7 copy.16
  (3 shorter events, 0.0 us)
Async XLA Ops:
  7.2 175.5 %copy-start = (bf16[1,1,1,64,128,128]{5,4,3,2,1,0:T(8,128)(2,1)S(1)}, bf16[1,1,1,64,128,128]{5,4,3,2,1,0:T(8,128)(2,1)}, u32[]{:S(2)}) copy-start(bf16[1,1,1,64,128,128]{5,4,3,2,1,0:T(8,128)(2,1)} %param.12) | copy-start | bytes 6291460
  7.2 164.4 %all-gather.3.cloned.1.call-start = ((), (), s32[]{:S(2)}) async-start(), calls=%async_computation.1 | async-start | bytes 8519680 | tf_op jit(solution)/shard_map/all_gather | solution.py:17
  7.9 242.1 %reduce-scatter.2.cloned.1.call-start = ((), (), s32[]{:S(2)}) async-start(), calls=%async_computation.2 | async-start | bytes 2359296 | tf_op jit(solution)/shard_map/reduce_scatter | solution.py:44
  207.0 6.3 copy-start.3
  210.6 2.7 copy-start.1
  213.3 36.7 %copy-start.2 = (bf16[256,256]{1,0:T(8,128)(2,1)S(1)}, bf16[256,256]{1,0:T(8,128)(2,1)}, u32[]{:S(2)}) copy-start(bf16[256,256]{1,0:T(8,128)(2,1)} %param.13) | copy-start | bytes 393220
  216.6 67.8 %all-gather.5.cloned.1.call-start = ((), (), s32[]{:S(2)}) async-start(), calls=%async_computation.3 | async-start | bytes 1179648 | tf_op jit(solution)/shard_map/all_gather | solution.py:52
  251.8 450.3 %all-reduce.2.cloned.1.call-start = ((), (), s32[]{:S(2)}) async-start(), calls=%async_computation.4 | async-start | bytes 3145728 | tf_op jit(solution)/shard_map/psum | solution.py:56
Sparse Core Ops, SparseCore 0:
  10.9 160.5 all-gather.2
  216.7 33.2 reduce-scatter.1
  252.7 31.6 all-gather.4
  290.6 411.4 all-reduce.1
where the time goes:
time: 712 us; the launch traced here: 711 us
  waiting for transfers between devices  639 us (90%)
  local copies, waits for them, and re-layouts  29.3 us (4%)
  matrix products  24.4 us (3%)
  between operations  14.5 us (2%)
    psum x1, waiting for transfers between devices, local(): grad_rel = lax.psum(weight_terms, ('dom', 'src'))  412 us
    all_gather x1, waiting for transfers between devices, local(): everyone = lax.all_gather(source_feats, 'dom', axis=0, tiled=True)  161 us
    reduce_scatter x1, waiting for transfers between devices, local(): lax.psum_scatter(jnp.einsum('rtd,rde->te', relation_terms, rel_weight, pr...  33.4 us
    all_gather x1, waiting for transfers between devices, local(): grad_rows = lax.all_gather(local_grad, ('src', 'rel'), axis=0, tiled=True)  32.6 us
  transfers between devices with their start and end apart: 4, of which 4 were waited for; matrix products, arithmetic and copies ran while one was open for 0% of the time, Pallas kernels for 0%

commit v1 on v0

--- a/solution.py
+++ b/solution.py
@@ -53,7 +53,7 @@
     weight_terms = jnp.einsum(
         "rtd,te->rde", relation_terms, grad_rows, preferred_element_type=jnp.float32
     )
-    grad_rel = lax.psum(weight_terms, ("dom", "src"))
+    grad_rel = lax.psum(lax.psum(weight_terms, "src"), "dom")
     return (out_feats, grad_rel)
 
 

time: 712 us -> 650 us (0.913)
  waiting for transfers between devices: 639 us -> 577 us
    psum x1 -> x2, waiting for transfers between devices: 412 us -> 350 us  [local(): grad_rel = lax.psum(lax.psum(weight_terms, 'src'), 'dom')]
  transfers between devices with their start and end apart: 4 -> 5, of which waited for: 4 -> 5; matrix products, arithmetic and copies ran while one was open for 0% -> 0% of each run, Pallas kernels for 0% -> 0%
where the time goes in v1:
time: 650 us
  waiting for transfers between devices  577 us (89%)
  local copies, waits for them, and re-layouts  29.3 us (5%)
  matrix products  24.4 us (4%)
  between operations  14.5 us (2%)
    psum x2, waiting for transfers between devices, local(): grad_rel = lax.psum(lax.psum(weight_terms, 'src'), 'dom')  350 us
    all_gather x1, waiting for transfers between devices, local(): everyone = lax.all_gather(source_feats, 'dom', axis=0, tiled=True)  161 us
    reduce_scatter x1, waiting for transfers between devices, local(): lax.psum_scatter(jnp.einsum('rtd,rde->te', relation_terms, rel_weight, pr...  33.4 us
    all_gather x1, waiting for transfers between devices, local(): grad_rows = lax.all_gather(local_grad, ('src', 'rel'), axis=0, tiled=True)  32.6 us
  transfers between devices with their start and end apart: 5, of which 5 were waited for; matrix products, arithmetic and copies ran while one was open for 0% of the time, Pallas kernels for 0%

profile of v1, /device:TPU:2, one launch (start us, length us, event | category | flops | bytes accessed | tf_op | source)
XLA Modules:
  0.0 649.6 jit_solution(5026396538015346244)
XLA Ops:
  7.2 0.0 copy-start
  7.2 0.0 all-gather.3.cloned.1.call-start
  7.2 0.7 all-gather.3.cloned.1.call-update
  7.9 0.0 reduce-scatter.2.cloned.1.call-start
  8.6 0.7 fusion.17
  9.3 0.7 add_bitcast_fusion
  10.0 0.7 fusion.18
  10.6 160.9 %all-gather.3.cloned.1.call-done = bf16[16384,256]{1,0:T(8,128)(2,1)} async-done(((bf16[256,256]{1,0:T(8,128)(2,1)}), bf16[16384,256]{1,0:T(8,128)(2,1)}) %all-gather.3.cloned.1.call-update) | async-done | bytes 8388624 | tf_op jit(solution)/shard_map/all_gather | solution.py:17
  171.5 6.2 gather_fusion
  177.7 4.9 gather_fusion.1
  182.6 0.0 copy-done
  182.6 6.7 %fusion.5 = f32[64,256,128]{2,1,0:T(8,128)} fusion(bf16[64,128,256]{2,1,0:T(8,128)(2,1)} %gather_fusion.1, bf16[1,1,1,64,128,128]{5,4,3,2,1,0:T(8,128)(2,1)S(1)} %copy-done), kind=kOutput, calls=%fused_computation.6 | convolution fusion | flops 536870912 | bytes 14680064 | tf_op jit(solution)/shard_map/eij,ejd->eid/dot_general | solution.py:27
  189.3 9.2 %copy.12 = f32[64,256,128]{1,0,2:T(8,128)} copy(f32[64,256,128]{2,1,0:T(8,128)} %fusion.5) | data formatting | bytes 16777216 | tf_op jit(solution)/shard_map/eij,ejd->eid/dot_general | solution.py:27
  198.5 8.4 %fusion.2 = bf16[96,128,256]{2,0,1:T(8,128)(2,1)S(1)} fusion(f32[64,256,128]{1,0,2:T(8,128)} %copy.12, s32[64]{0:T(128)S(1)} %add_bitcast_fusion, pred[64]{0:T(512)(128)(4,1)S(1)} %iota_compare_fusion.1), kind=kOutput, calls=%fused_computation.4 | convolution fusion | flops 2419077120 | bytes 14680384 | tf_op jit(solution)/shard_map/se,eid->sid/dot_general | solution.py:34
  207.0 0.0 copy-start.3
  207.0 3.7 copy.10
  210.6 2.6 copy-done.1
  213.3 3.3 convolution_bitcast_fusion
  216.5 0.0 reduce-scatter.2.cloned.1.call-update
  216.6 0.0 all-gather.5.cloned.1.call-start
  216.6 33.4 %reduce-scatter.2.cloned.1.call-done = f32[256,256]{1,0:T(8,128)} async-done(((f32[2048,256]{1,0:T(8,128)}), f32[256,256]{1,0:T(8,128)}) %reduce-scatter.2.cloned.1.call-update) | async-done | bytes 262160 | tf_op jit(solution)/shard_map/reduce_scatter | solution.py:44
  250.0 1.8 multiply_convert_fusion
  251.7 0.0 all-gather.5.cloned.1.call-update
  251.8 0.0 all-reduce.3.cloned.1.call-start
  251.8 32.6 %all-gather.5.cloned.1.call-done = bf16[2048,256]{1,0:T(8,128)(2,1)} async-done(((bf16[256,256]{1,0:T(8,128)(2,1)}), bf16[2048,256]{1,0:T(8,128)(2,1)}) %all-gather.5.cloned.1.call-update) | async-done | bytes 1048592 | tf_op jit(solution)/shard_map/all_gather | solution.py:52
  284.4 6.0 fusion.7
  290.4 0.0 all-reduce.3.cloned.1.call-update
  290.4 0.0 all-reduce.5.cloned.1.call-start
  290.5 66.1 %all-reduce.3.cloned.1.call-done = f32[6,256,256]{2,1,0:T(8,128)} async-done(((f32[6,256,256]{2,1,0:T(8,128)}), f32[6,256,256]{2,1,0:T(8,128)}) %all-reduce.3.cloned.1.call-update) | async-done | bytes 1572880 | tf_op jit(solution)/shard_map/psum | solution.py:56
  356.6 0.0 all-reduce.5.cloned.1.call-update
  356.6 283.7 %all-reduce.5.cloned.1.call-done = f32[6,256,256]{2,1,0:T(8,128)} async-done(((f32[6,256,256]{2,1,0:T(8,128)}), f32[6,256,256]{2,1,0:T(8,128)}) %all-reduce.5.cloned.1.call-update) | async-done | bytes 1572880 | tf_op jit(solution)/shard_map/psum | solution.py:56
  640.3 2.7 copy.17
  (6 shorter events, 0.0 us)
Async XLA Ops:
  7.2 175.5 %copy-start = (bf16[1,1,1,64,128,128]{5,4,3,2,1,0:T(8,128)(2,1)S(1)}, bf16[1,1,1,64,128,128]{5,4,3,2,1,0:T(8,128)(2,1)}, u32[]{:S(2)}) copy-start(bf16[1,1,1,64,128,128]{5,4,3,2,1,0:T(8,128)(2,1)} %param.12) | copy-start | bytes 6291460
  7.2 164.4 %all-gather.3.cloned.1.call-start = ((), (), s32[]{:S(2)}) async-start(), calls=%async_computation.1 | async-start | bytes 8519680 | tf_op jit(solution)/shard_map/all_gather | solution.py:17
  7.9 242.1 %reduce-scatter.2.cloned.1.call-start = ((), (), s32[]{:S(2)}) async-start(), calls=%async_computation.2 | async-start | bytes 2359296 | tf_op jit(solution)/shard_map/reduce_scatter | solution.py:44
  207.0 6.3 copy-start.3
  210.6 2.7 copy-start.1
  213.3 36.7 %copy-start.2 = (bf16[256,256]{1,0:T(8,128)(2,1)S(1)}, bf16[256,256]{1,0:T(8,128)(2,1)}, u32[]{:S(2)}) copy-start(bf16[256,256]{1,0:T(8,128)(2,1)} %param.13) | copy-start | bytes 393220
  216.6 67.8 %all-gather.5.cloned.1.call-start = ((), (), s32[]{:S(2)}) async-start(), calls=%async_computation.3 | async-start | bytes 1179648 | tf_op jit(solution)/shard_map/all_gather | solution.py:52
  251.8 104.8 %all-reduce.3.cloned.1.call-start = ((), (), s32[]{:S(2)}) async-start(), calls=%async_computation.4 | async-start | bytes 3145728 | tf_op jit(solution)/shard_map/psum | solution.py:56
  290.4 349.9 %all-reduce.5.cloned.1.call-start = ((), (), s32[]{:S(2)}) async-start(), calls=%async_computation.5 | async-start | bytes 3145728 | tf_op jit(solution)/shard_map/psum | solution.py:56
Sparse Core Ops, SparseCore 0:
  10.9 160.5 all-gather.2
  216.7 33.2 reduce-scatter.1
  252.7 31.6 all-gather.4
  290.6 65.9 all-reduce.2
  359.9 280.4 all-reduce.4
